TPU v7x, 32 devices: a whole 2x2x4 slice. The times are simulated.
32 devices in a mesh: pix: 8 (over y, x, core), tm: 4 (over z).
Axes of the slice: x: 2, y: 2, z: 4, core: 2. Of those that a mesh axis runs over, the one named last changes fastest.
Arguments:
- raw_movie: float32 [64, 256, 2048], P('pix', None, 'tm'), may hold values from 0.05 to 2
- footprints: float32 [256, 16384], P('tm', 'pix'), may hold values from 0.05 to 1
- traces: float32 [256, 2048], P('pix', 'tm'), may hold values from 0.05 to 1
Outputs:
- denoised: float32 [64, 256, 2048], P('pix', None, 'tm')
- new_footprints: float32 [256, 16384], P('tm', 'pix')
- new_traces: float32 [256, 2048], P('pix', 'tm')
All inputs are finite; a program needn't handle non-finite values.
Results may differ from a plain program's by a relative error of at most 0.00013.
Values sent between devices are 32-bit elements; how exact they have to be, the bound alone decides.
No kernel may reach another device: no remote copies, remote signals or barrier semaphores. Data moves between devices by JAX's collectives and lax.ppermute only.
A program may use at most 64 MiB of HBM per device.

v0:
```python
import jax
import jax.numpy as jnp
from jax import lax
from jax.sharding import PartitionSpec as P

edge_scale = 0.5
step_size = 0.24


def with_halo(cells, sides, width):
    for axis, dim in sides:
        count = lax.axis_size(axis)
        ends = count - 1
        head = lax.slice_in_dim(cells, 0, width, axis=dim)
        tail = lax.slice_in_dim(cells, cells.shape[dim] - width, cells.shape[dim], axis=dim)
        cells = jnp.concatenate(
            [
                lax.ppermute(tail, axis, [(i, (i + 1) % count) for i in range(ends)]),
                cells,
                lax.ppermute(head, axis, [((i + 1) % count, i) for i in range(ends)]),
            ],
            axis=dim,
        )
    return cells


def flux_term(change):
    return change / (1.0 + change / edge_scale * (change / edge_scale))


def substep(extended):
    middle = extended[1:-1]
    padded = jnp.pad(middle, ((0, 0), (1, 1), (0, 0)))
    summed = flux_term(extended[:-2] - middle) + flux_term(extended[2:] - middle)
    summed = summed + flux_term(padded[:, :-2] - middle) + flux_term(padded[:, 2:] - middle)
    return middle + step_size * summed


def matmul_hi(left, right):
    return jnp.dot(left, right, precision=lax.Precision.HIGHEST, preferred_element_type=jnp.float32)


def contract_last(left, right):
    return lax.dot_general(
        left,
        right,
        (((1,), (1,)), ((), ())),
        precision=lax.Precision.HIGHEST,
        preferred_element_type=jnp.float32,
    )


def body(raw_movie, footprints, traces):
    row_count = raw_movie.shape[0]
    col_count = raw_movie.shape[1]
    frame_count = raw_movie.shape[2]
    current = raw_movie
    for repeat in range(4):
        extended = with_halo(current, (("pix", 0),), 1)
        current = substep(extended)
    pixels = current.reshape(row_count * col_count, frame_count)
    foot_full = lax.all_gather(footprints, "tm", axis=0, tiled=True)
    trace_full = lax.all_gather(traces, "pix", axis=0, tiled=True)
    part = foot_full
    merged = lax.psum_scatter(
        jnp.concatenate([matmul_hi(part, pixels), contract_last(part, foot_full)], axis=1),
        "pix",
        scatter_dimension=0,
        tiled=True,
    )
    numerator = merged[:, :frame_count]
    gram_rows = merged[:, frame_count:]
    new_traces = traces * numerator / matmul_hi(gram_rows, trace_full)
    new_full = lax.all_gather(new_traces, "pix", axis=0, tiled=True)
    part = new_full
    joined = lax.psum_scatter(
        jnp.concatenate([contract_last(part, pixels), contract_last(part, new_full)], axis=1),
        "tm",
        scatter_dimension=0,
        tiled=True,
    )
    foot_numerator = joined[:, : row_count * col_count]
    trace_rows = joined[:, row_count * col_count :]
    new_footprints = footprints * foot_numerator / matmul_hi(trace_rows, foot_full)
    return (current, new_footprints, new_traces)


def solution(mesh):
    placed = (P("pix", None, "tm"), P("tm", "pix"), P("pix", "tm"))
    return jax.shard_map(
        body,
        mesh=mesh,
        in_specs=placed,
        out_specs=(P("pix", None, "tm"), P("tm", "pix"), P("pix", "tm")),
        check_vma=False,
    )
```

profile of v0, /device:TPU:0, one launch (start us, length us, event | category | flops | bytes accessed | tf_op | source)
XLA Modules:
  0.0 233.4 jit_solution(9281021780774878681)
XLA Ops:
  7.2 0.0 all-gather.2.cloned.1.call-start
  7.2 1.3 fusion.13
  8.5 2.4 %collective-permute-start = (f32[1,256,512]{2,1,0:T(8,128)S(1)}, f32[1,256,512]{2,1,0:T(8,128)S(1)}, u32[]{:S(2)}, u32[]{:S(2)}) collective-permute-start(f32[1,256,512]{2,1,0:T(8,128)S(1)} %get-tuple-element.12), channel_id=1, source_target_pairs={{0,4},{4,8},{8,12},{12,16},{16,20},{20,24},{24,28},{1,5},{5,9},{9,... | collective-permute-start | bytes 1572872 | tf_op jit(solution)/shard_map/ppermute | solution.py:18
  10.9 1.3 collective-permute-start.1
  12.2 0.2 collective-permute-done
  12.4 4.4 %collective-permute-done.1 = f32[1,256,512]{2,1,0:T(8,128)S(1)} collective-permute-done((f32[1,256,512]{2,1,0:T(8,128)S(1)}, f32[1,256,512]{2,1,0:T(8,128)S(1)}, u32[]{:S(2)}, u32[]{:S(2)}) %collective-permute-start.1) | collective-permute-done | bytes 524320 | tf_op jit(solution)/shard_map/ppermute | solution.py:20
  16.8 9.8 %multiply_add_fusion.3 = f32[8,256,512]{2,1,0:T(8,128)S(1)} fusion(f32[8,256,512]{2,1,0:T(8,128)} %param.3, f32[1,256,512]{2,1,0:T(8,128)S(1)} %collective-permute-done.1, f32[1,256,512]{2,1,0:T(8,128)S(1)} %collective-permute-done), kind=kLoop, calls=%fused_computation.19 | loop fusion | flops 28311552 | bytes 9437184 | tf_op jit(solution)/shard_map/add | solution.py:36
  26.6 0.1 fusion.12
  26.7 12.0 %collective-permute-start.2 = (f32[1,256,512]{2,1,0:T(8,128)S(1)}, f32[1,256,512]{2,1,0:T(8,128)S(1)}, u32[]{:S(2)}, u32[]{:S(2)}) collective-permute-start(f32[1,256,512]{2,1,0:T(8,128)S(1)} %get-tuple-element.10), channel_id=1, source_target_pairs={{0,4},{4,8},{8,12},{12,16},{16,20},{20,24},{24,28},{1,5},{5,9},{9,... | collective-permute-start | bytes 1572872 | tf_op jit(solution)/shard_map/ppermute | solution.py:18
  38.7 1.3 collective-permute-start.3
  40.0 0.2 collective-permute-done.2
  40.2 2.3 collective-permute-done.3
  42.5 4.5 %multiply_add_fusion.2 = f32[8,256,512]{2,1,0:T(8,128)S(1)} fusion(f32[8,256,512]{2,1,0:T(8,128)S(1)} %multiply_add_fusion.3, f32[1,256,512]{2,1,0:T(8,128)S(1)} %collective-permute-done.3, f32[1,256,512]{2,1,0:T(8,128)S(1)} %collective-permute-done.2), kind=kLoop, calls=%fused_computation.18 | loop fusion | flops 28311552 | bytes 9437184 | tf_op jit(solution)/shard_map/add | solution.py:36
  47.0 0.0 copy-start.2
  47.1 2.0 copy-done.2
  49.1 0.1 fusion.11
  49.1 11.5 %collective-permute-start.4 = (f32[1,256,512]{2,1,0:T(8,128)S(1)}, f32[1,256,512]{2,1,0:T(8,128)S(1)}, u32[]{:S(2)}, u32[]{:S(2)}) collective-permute-start(f32[1,256,512]{2,1,0:T(8,128)S(1)} %get-tuple-element.8), channel_id=1, source_target_pairs={{0,4},{4,8},{8,12},{12,16},{16,20},{20,24},{24,28},{1,5},{5,9},{9,... | collective-permute-start | bytes 1572872 | tf_op jit(solution)/shard_map/ppermute | solution.py:18
  60.6 1.3 collective-permute-start.5
  61.9 0.0 all-gather.2.cloned.1.call-update
  62.0 0.0 reduce-scatter.7.cloned.1.call-start
  62.0 0.1 collective-permute-done.4
  62.1 2.3 collective-permute-done.5
  64.4 10.0 %multiply_add_fusion.1 = f32[8,256,512]{2,1,0:T(8,128)S(1)} fusion(f32[8,256,512]{2,1,0:T(8,128)} %copy-done.2, f32[1,256,512]{2,1,0:T(8,128)S(1)} %collective-permute-done.5, f32[1,256,512]{2,1,0:T(8,128)S(1)} %collective-permute-done.4), kind=kLoop, calls=%fused_computation.17 | loop fusion | flops 28311552 | bytes 9437184 | tf_op jit(solution)/shard_map/add | solution.py:36
  74.4 0.1 fusion.10
  74.5 10.5 %collective-permute-start.6 = (f32[1,256,512]{2,1,0:T(8,128)S(1)}, f32[1,256,512]{2,1,0:T(8,128)S(1)}, u32[]{:S(2)}, u32[]{:S(2)}) collective-permute-start(f32[1,256,512]{2,1,0:T(8,128)S(1)} %get-tuple-element.6), channel_id=1, source_target_pairs={{0,4},{4,8},{8,12},{12,16},{16,20},{20,24},{24,28},{1,5},{5,9},{9,... | collective-permute-start | bytes 1572872 | tf_op jit(solution)/shard_map/ppermute | solution.py:18
  85.0 1.5 collective-permute-start.7
  86.5 0.0 collective-permute-done.6
  86.5 2.3 collective-permute-done.7
  88.8 5.5 %multiply_add_fusion = f32[8,256,512]{2,1,0:T(8,128)} fusion(f32[8,256,512]{2,1,0:T(8,128)S(1)} %multiply_add_fusion.1, f32[1,256,512]{2,1,0:T(8,128)S(1)} %collective-permute-done.7, f32[1,256,512]{2,1,0:T(8,128)S(1)} %collective-permute-done.6), kind=kLoop, calls=%fused_computation.16 | loop fusion | flops 28311552 | bytes 9437184 | tf_op jit(solution)/shard_map/add | solution.py:36
  94.3 14.5 %all-gather.2.cloned.1.call-done = f32[256,2048]{1,0:T(8,128)} async-done(((f32[64,2048]{1,0:T(8,128)}), f32[256,2048]{1,0:T(8,128)}) %all-gather.2.cloned.1.call-update) | async-done | bytes 2097168 | tf_op jit(solution)/shard_map/all_gather | solution.py:62
  108.8 0.0 copy-start
  108.8 4.2 %fusion.14 = f32[256,256]{0,1:T(8,128)S(1)} fusion(f32[256,2048]{1,0:T(8,128)} %all-gather.2.cloned.1.call-done), kind=kOutput, calls=%fused_computation.33 | convolution fusion | flops 1610612736 | bytes 2359296 | tf_op jit(solution)/shard_map/dot_general | solution.py:44
  113.0 0.0 copy-done
  113.0 0.0 copy-start.4
  113.1 8.4 %convolution_bitcast_fusion = f32[256,512]{0,1:T(8,128)S(1)} fusion(f32[2048,512]{1,0:T(8,128)S(1)} %bitcast.15, f32[256,2048]{1,0:T(8,128)} %all-gather.2.cloned.1.call-done), kind=kOutput, calls=%fused_computation.22 | convolution fusion | flops 3221225472 | bytes 6815744 | tf_op jit(solution)/shard_map/dot_general | solution.py:40
  121.5 0.1 pad_maximum_fusion.9
  121.6 1.1 copy.13
  122.7 0.0 reduce-scatter.7.cloned.1.call-update
  122.7 0.0 reduce-scatter.5.cloned.1.call-start
  122.8 0.0 copy-done.4
  122.8 9.8 %all_gather.10 = f32[256,512]{1,0:T(8,128)S(1)} all-gather(f32[32,512]{1,0:T(8,128)S(1)} %copy-done.4), channel_id=1, replica_groups=mesh['pix'=8,'tm'=4] {'pix'}, dimensions={0}, use_global_device_ids=true | all-gather | bytes 589824 | tf_op jit(solution)/shard_map/all_gather | solution.py:63
  132.6 24.0 %reduce-scatter.7.cloned.1.call-done = f32[32,768]{1,0:T(8,128)} async-done(((f32[256,768]{1,0:T(8,128)}), f32[32,768]{1,0:T(8,128)}) %reduce-scatter.7.cloned.1.call-update) | async-done | bytes 98320 | tf_op jit(solution)/shard_map/reduce_scatter | solution.py:65
  156.7 1.3 convolution_divide_fusion.1
  157.9 0.0 copy-start.5
  157.9 10.0 %all_gather.11 = f32[256,512]{1,0:T(8,128)S(1)} all-gather(f32[32,512]{1,0:T(8,128)S(1)} %convolution_divide_fusion.1), channel_id=1, replica_groups=mesh['pix'=8,'tm'=4] {'pix'}, dimensions={0}, use_global_device_ids=true | all-gather | bytes 589824 | tf_op jit(solution)/shard_map/all_gather | solution.py:74
  168.0 5.5 %fusion.15 = f32[256,2048]{1,0:T(8,128)S(1)} fusion(f32[256,512]{1,0:T(8,128)S(1)} %all_gather.11, f32[2048,512]{1,0:T(8,128)} %bitcast.14), kind=kOutput, calls=%fused_computation.34 | convolution fusion | flops 3221225472 | bytes 6815744 | tf_op jit(solution)/shard_map/dot_general | solution.py:44
  173.5 0.0 copy-start.1
  173.5 0.0 copy-start.3
  173.5 0.6 fusion.16
  174.1 0.0 copy-done.5
  174.1 1.6 pad_maximum_fusion.8
  175.7 0.0 reduce-scatter.5.cloned.1.call-update
  175.8 47.9 %reduce-scatter.5.cloned.1.call-done = f32[64,2304]{1,0:T(8,128)} async-done(((f32[256,2304]{1,0:T(8,128)}), f32[64,2304]{1,0:T(8,128)}) %reduce-scatter.5.cloned.1.call-update) | async-done | bytes 589840 | tf_op jit(solution)/shard_map/reduce_scatter | solution.py:76
  223.6 0.0 copy-done.1
  223.6 0.0 copy-done.3
  223.6 3.3 %convolution_divide_fusion = f32[64,2048]{1,0:T(8,128)} fusion(f32[256,2048]{1,0:T(8,128)S(1)} %copy-done.1, f32[64,2048]{1,0:T(8,128)S(1)} %copy-done.3, f32[64,2304]{1,0:T(8,128)} %reduce-scatter.5.cloned.1.call-done), kind=kOutput, calls=%fused_computation.21 | convolution fusion | flops 402915328 | bytes 3735552 | tf_op jit(solution)/shard_map/dot_general | solution.py:40
Async XLA Ops:
  7.2 101.6 %all-gather.2.cloned.1.call-start = ((), (), s32[]{:S(2)}) async-start(), calls=%async_computation.2 | async-start | bytes 2621440 | tf_op jit(solution)/shard_map/all_gather | solution.py:62
  8.5 3.9 %collective-permute-start = (f32[1,256,512]{2,1,0:T(8,128)S(1)}, f32[1,256,512]{2,1,0:T(8,128)S(1)}, u32[]{:S(2)}, u32[]{:S(2)}) collective-permute-start(f32[1,256,512]{2,1,0:T(8,128)S(1)} %get-tuple-element.12), channel_id=1, source_target_pairs={{0,4},{4,8},{8,12},{12,16},{16,20},{20,24},{24,28},{1,5},{5,9},{9,... | collective-permute-start | bytes 1572872 | tf_op jit(solution)/shard_map/ppermute | solution.py:18
  10.9 5.9 %collective-permute-start.1 = (f32[1,256,512]{2,1,0:T(8,128)S(1)}, f32[1,256,512]{2,1,0:T(8,128)S(1)}, u32[]{:S(2)}, u32[]{:S(2)}) collective-permute-start(f32[1,256,512]{2,1,0:T(8,128)S(1)} %get-tuple-element.13), channel_id=1, source_target_pairs={{4,0},{8,4},{12,8},{16,12},{20,16},{24,20},{28,24},{5,1},{9,5},{13... | collective-permute-start | bytes 1572872 | tf_op jit(solution)/shard_map/ppermute | solution.py:20
  26.7 13.5 %collective-permute-start.2 = (f32[1,256,512]{2,1,0:T(8,128)S(1)}, f32[1,256,512]{2,1,0:T(8,128)S(1)}, u32[]{:S(2)}, u32[]{:S(2)}) collective-permute-start(f32[1,256,512]{2,1,0:T(8,128)S(1)} %get-tuple-element.10), channel_id=1, source_target_pairs={{0,4},{4,8},{8,12},{12,16},{16,20},{20,24},{24,28},{1,5},{5,9},{9,... | collective-permute-start | bytes 1572872 | tf_op jit(solution)/shard_map/ppermute | solution.py:18
  38.7 3.8 %collective-permute-start.3 = (f32[1,256,512]{2,1,0:T(8,128)S(1)}, f32[1,256,512]{2,1,0:T(8,128)S(1)}, u32[]{:S(2)}, u32[]{:S(2)}) collective-permute-start(f32[1,256,512]{2,1,0:T(8,128)S(1)} %get-tuple-element.11), channel_id=1, source_target_pairs={{4,0},{8,4},{12,8},{16,12},{20,16},{24,20},{28,24},{5,1},{9,5},{13... | collective-permute-start | bytes 1572872 | tf_op jit(solution)/shard_map/ppermute | solution.py:20
  47.0 2.0 copy-start.2
  49.1 13.0 %collective-permute-start.4 = (f32[1,256,512]{2,1,0:T(8,128)S(1)}, f32[1,256,512]{2,1,0:T(8,128)S(1)}, u32[]{:S(2)}, u32[]{:S(2)}) collective-permute-start(f32[1,256,512]{2,1,0:T(8,128)S(1)} %get-tuple-element.8), channel_id=1, source_target_pairs={{0,4},{4,8},{8,12},{12,16},{16,20},{20,24},{24,28},{1,5},{5,9},{9,... | collective-permute-start | bytes 1572872 | tf_op jit(solution)/shard_map/ppermute | solution.py:18
  60.6 3.8 %collective-permute-start.5 = (f32[1,256,512]{2,1,0:T(8,128)S(1)}, f32[1,256,512]{2,1,0:T(8,128)S(1)}, u32[]{:S(2)}, u32[]{:S(2)}) collective-permute-start(f32[1,256,512]{2,1,0:T(8,128)S(1)} %get-tuple-element.9), channel_id=1, source_target_pairs={{4,0},{8,4},{12,8},{16,12},{20,16},{24,20},{28,24},{5,1},{9,5},{13... | collective-permute-start | bytes 1572872 | tf_op jit(solution)/shard_map/ppermute | solution.py:20
  62.0 94.7 %reduce-scatter.7.cloned.1.call-start = ((), (), s32[]{:S(2)}) async-start(), calls=%async_computation.4 | async-start | bytes 884736 | tf_op jit(solution)/shard_map/reduce_scatter | solution.py:65
  74.5 12.0 %collective-permute-start.6 = (f32[1,256,512]{2,1,0:T(8,128)S(1)}, f32[1,256,512]{2,1,0:T(8,128)S(1)}, u32[]{:S(2)}, u32[]{:S(2)}) collective-permute-start(f32[1,256,512]{2,1,0:T(8,128)S(1)} %get-tuple-element.6), channel_id=1, source_target_pairs={{0,4},{4,8},{8,12},{12,16},{16,20},{20,24},{24,28},{1,5},{5,9},{9,... | collective-permute-start | bytes 1572872 | tf_op jit(solution)/shard_map/ppermute | solution.py:18
  85.0 3.8 %collective-permute-start.7 = (f32[1,256,512]{2,1,0:T(8,128)S(1)}, f32[1,256,512]{2,1,0:T(8,128)S(1)}, u32[]{:S(2)}, u32[]{:S(2)}) collective-permute-start(f32[1,256,512]{2,1,0:T(8,128)S(1)} %get-tuple-element.7), channel_id=1, source_target_pairs={{4,0},{8,4},{12,8},{16,12},{20,16},{24,20},{28,24},{5,1},{9,5},{13... | collective-permute-start | bytes 1572872 | tf_op jit(solution)/shard_map/ppermute | solution.py:20
  108.8 4.2 %copy-start = (f32[8,256,512]{2,1,0:T(8,128)S(1)}, f32[8,256,512]{2,1,0:T(8,128)}, u32[]{:S(2)}) copy-start(f32[8,256,512]{2,1,0:T(8,128)} %multiply_add_fusion) | copy-start | bytes 12582916
  113.0 9.7 %copy-start.4 = (f32[32,512]{1,0:T(8,128)S(1)}, f32[32,512]{1,0:T(8,128)}, u32[]{:S(2)}) copy-start(f32[32,512]{1,0:T(8,128)} %param.5) | copy-start | bytes 196612
  122.7 100.9 %reduce-scatter.5.cloned.1.call-start = ((), (), s32[]{:S(2)}) async-start(), calls=%async_computation.3 | async-start | bytes 2949120 | tf_op jit(solution)/shard_map/reduce_scatter | solution.py:76
  157.9 16.2 %copy-start.5 = (f32[32,512]{1,0:T(8,128)}, f32[32,512]{1,0:T(8,128)S(1)}, u32[]{:S(2)}) copy-start(f32[32,512]{1,0:T(8,128)S(1)} %convolution_divide_fusion.1) | copy-start | bytes 196612
  173.5 50.1 %copy-start.1 = (f32[256,2048]{1,0:T(8,128)S(1)}, f32[256,2048]{1,0:T(8,128)}, u32[]{:S(2)}) copy-start(f32[256,2048]{1,0:T(8,128)} %all-gather.2.cloned.1.call-done) | copy-start | bytes 6291460
  173.5 50.1 %copy-start.3 = (f32[64,2048]{1,0:T(8,128)S(1)}, f32[64,2048]{1,0:T(8,128)}, u32[]{:S(2)}) copy-start(f32[64,2048]{1,0:T(8,128)} %param.4) | copy-start | bytes 1572868
Sparse Core Ops, SparseCore 0:
  62.1 46.6 all-gather.1
  122.9 33.7 reduce-scatter.6
  175.9 47.6 reduce-scatter.4
where the time goes:
time: 234 us; the launch traced here: 233 us
  waiting for transfers between devices  98.3 us (42%)
  starting transfers between devices  41.9 us (18%)
  other arithmetic  31.5 us (13%)
  matrix products  23.3 us (10%)
  blocking collectives  19.8 us (8%)
  between operations  14 us (6%)
  local copies, waits for them, and re-layouts  4.67 us (2%)
    reduce_scatter x1, waiting for transfers between devices, body(): lax.psum_scatter(jnp.concatenate([contract_last(part, pixels), contract_l...  47.9 us
    ppermute x4, starting transfers between devices, with_halo(): lax.ppermute(tail, axis, [(i, (i + 1) % count) for i in range(ends)])  36.4 us
    add x4, other arithmetic, substep(): return middle + step_size * summed  29.8 us
    reduce_scatter x1, waiting for transfers between devices, body(): lax.psum_scatter(jnp.concatenate([matmul_hi(part, pixels), contract_last(...  24 us
    all_gather x1, waiting for transfers between devices, body(): foot_full = lax.all_gather(footprints, 'tm', axis=0, tiled=True)  14.5 us
    dot_general x3, matrix products, matmul_hi(): jnp.dot(left, right, precision=lax.Precision.HIGHEST, preferred_element_t...  13 us
    ppermute x4, waiting for transfers between devices, with_halo(): lax.ppermute(head, axis, [((i + 1) % count, i) for i in range(ends)])  11.3 us
    dot_general x3, matrix products, contract_last(): lax.dot_general(left, right, (((1,), (1,)), ((), ())), precision=lax.Prec...  10.3 us
  transfers between devices with their start and end apart: 11, of which 10 were waited for; matrix products, arithmetic and copies ran while one was open for 7% of the time, Pallas kernels for 0%

commit v1 on v0

--- a/solution.py
+++ b/solution.py
@@ -59,7 +59,13 @@
         extended = with_halo(current, (("pix", 0),), 1)
         current = substep(extended)
     pixels = current.reshape(row_count * col_count, frame_count)
-    foot_full = lax.all_gather(footprints, "tm", axis=0, tiled=True)
+    size = lax.axis_size("tm")
+    held, blocks = (footprints, [footprints])
+    for _ in range(size - 1):
+        held = lax.ppermute(held, "tm", [(i_2, (i_2 + 1) % size) for i_2 in range(size)])
+        blocks.insert(0, held)
+    line = jnp.concatenate(blocks, axis=0)
+    foot_full = jnp.roll(line, (lax.axis_index("tm") + 1) * footprints.shape[0], axis=0)
     trace_full = lax.all_gather(traces, "pix", axis=0, tiled=True)
     part = foot_full
     merged = lax.psum_scatter(

time: 234 us -> 221 us (0.944)
  waiting for transfers between devices: 98.3 us -> 73.4 us
  blocking collectives: 19.8 us -> 36.6 us
  matrix products: 23.3 us -> 16.8 us
    all_gather x1, blocking collectives: 9.81 us -> 26.5 us  [body(): trace_full = lax.all_gather(traces, 'pix', axis=0, tiled=True)]
    all_gather x1 -> x0, waiting for transfers between devices: 14.5 us -> none  [body(): foot_full = lax.all_gather(footprints, 'tm', axis=0, tiled=True)]
    ppermute x4, waiting for transfers between devices: 11.3 us -> 0.01 us  [with_halo(): lax.ppermute(head, axis, [((i + 1) % count, i) for i in range(ends)])]
    ppermute x0 -> x3, starting transfers between devices: none -> 6.36 us  [body(): lax.ppermute(held, 'tm', [(i_2, (i_2 + 1) % size) for i_2 in range(size)])]
    ppermute x4, starting transfers between devices: 36.4 us -> 30.6 us  [with_halo(): lax.ppermute(tail, axis, [(i, (i + 1) % count) for i in range(ends)])]
    dot_general x3, matrix products: 13 us -> 8.83 us  [matmul_hi(): jnp.dot(left, right, precision=lax.Precision.HIGHEST, preferred_element_t...]
  transfers between devices with their start and end apart: 11 -> 13, of which waited for: 10 -> 2; matrix products, arithmetic and copies ran while one was open for 7% -> 12% of each run, Pallas kernels for 0% -> 0%
where the time goes in v1:
time: 221 us
  waiting for transfers between devices  73.4 us (33%)
  starting transfers between devices  42.3 us (19%)
  blocking collectives  36.6 us (17%)
  other arithmetic  31.5 us (14%)
  matrix products  16.8 us (8%)
  between operations  14.4 us (7%)
  local copies, waits for them, and re-layouts  5.8 us (3%)
    reduce_scatter x1, waiting for transfers between devices, body(): lax.psum_scatter(jnp.concatenate([contract_last(part, pixels), contract_l...  47.8 us
    ppermute x4, starting transfers between devices, with_halo(): lax.ppermute(tail, axis, [(i, (i + 1) % count) for i in range(ends)])  30.6 us
    add x4, other arithmetic, substep(): return middle + step_size * summed  28.9 us
    all_gather x1, blocking collectives, body(): trace_full = lax.all_gather(traces, 'pix', axis=0, tiled=True)  26.5 us
    reduce_scatter x1, waiting for transfers between devices, body(): lax.psum_scatter(jnp.concatenate([matmul_hi(part, pixels), contract_last(...  25.6 us
    all_gather x1, blocking collectives, body(): new_full = lax.all_gather(new_traces, 'pix', axis=0, tiled=True)  10 us
    dot_general x3, matrix products, matmul_hi(): jnp.dot(left, right, precision=lax.Precision.HIGHEST, preferred_element_t...  8.83 us
    dot_general x3, matrix products, contract_last(): lax.dot_general(left, right, (((1,), (1,)), ((), ())), precision=lax.Prec...  8 us
  transfers between devices with their start and end apart: 13, of which 2 were waited for; matrix products, arithmetic and copies ran while one was open for 12% of the time, Pallas kernels for 0%

profile of v1, /device:TPU:0, one launch (start us, length us, event | category | flops | bytes accessed | tf_op | source)
XLA Modules:
  0.0 220.8 jit_solution(3521267773429894203)
XLA Ops:
  7.2 0.0 reduce-scatter.3.cloned.1.call-start
  7.2 1.3 fusion.21
  8.5 1.3 collective-permute-start.1
  9.8 3.1 %collective-permute-start = (f32[1,256,512]{2,1,0:T(8,128)S(1)}, f32[1,256,512]{2,1,0:T(8,128)S(1)}, u32[]{:S(2)}, u32[]{:S(2)}) collective-permute-start(f32[1,256,512]{2,1,0:T(8,128)S(1)} %get-tuple-element.9), channel_id=1, source_target_pairs={{0,4},{4,8},{8,12},{12,16},{16,20},{20,24},{24,28},{1,5},{5,9},{9,... | collective-permute-start | bytes 1572872 | tf_op jit(solution)/shard_map/ppermute | solution.py:18
  12.9 3.1 %collective-permute-start.8 = (f32[64,2048]{1,0:T(8,128)}, f32[64,2048]{1,0:T(8,128)S(1)}, u32[]{:S(2)}, u32[]{:S(2)}) collective-permute-start(f32[64,2048]{1,0:T(8,128)} %param.4), channel_id=1, source_target_pairs={{0,1},{1,2},{2,3},{3,0},{4,5},{5,6},{6,7},{7,4},{8,9},{9,10},{10,1... | collective-permute-start | bytes 1572872 | tf_op jit(solution)/shard_map/ppermute | solution.py:65
  16.0 0.0 collective-permute-done.1
  16.0 0.0 collective-permute-done
  16.0 9.8 %multiply_add_fusion.3 = f32[8,256,512]{2,1,0:T(8,128)S(1)} fusion(f32[8,256,512]{2,1,0:T(8,128)} %param.3, f32[1,256,512]{2,1,0:T(8,128)S(1)} %collective-permute-done.1, f32[1,256,512]{2,1,0:T(8,128)S(1)} %collective-permute-done), kind=kLoop, calls=%fused_computation.19 | loop fusion | flops 28311552 | bytes 9437184 | tf_op jit(solution)/shard_map/add | solution.py:36
  25.8 0.1 fusion.20
  25.9 1.3 collective-permute-start.3
  27.2 9.1 %collective-permute-start.2 = (f32[1,256,512]{2,1,0:T(8,128)S(1)}, f32[1,256,512]{2,1,0:T(8,128)S(1)}, u32[]{:S(2)}, u32[]{:S(2)}) collective-permute-start(f32[1,256,512]{2,1,0:T(8,128)S(1)} %get-tuple-element.7), channel_id=1, source_target_pairs={{0,4},{4,8},{8,12},{12,16},{16,20},{20,24},{24,28},{1,5},{5,9},{9,... | collective-permute-start | bytes 1572872 | tf_op jit(solution)/shard_map/ppermute | solution.py:18
  36.3 0.0 collective-permute-done.8
  36.3 1.6 collective-permute-start.9
  38.0 0.0 collective-permute-done.3
  38.0 0.0 collective-permute-done.2
  38.0 4.5 %multiply_add_fusion.2 = f32[8,256,512]{2,1,0:T(8,128)S(1)} fusion(f32[8,256,512]{2,1,0:T(8,128)S(1)} %multiply_add_fusion.3, f32[1,256,512]{2,1,0:T(8,128)S(1)} %collective-permute-done.3, f32[1,256,512]{2,1,0:T(8,128)S(1)} %collective-permute-done.2), kind=kLoop, calls=%fused_computation.18 | loop fusion | flops 28311552 | bytes 9437184 | tf_op jit(solution)/shard_map/add | solution.py:36
  42.5 0.0 copy-start.1
  42.5 2.0 copy-done.1
  44.5 0.1 fusion.19
  44.6 1.3 collective-permute-start.5
  45.9 8.7 %collective-permute-start.4 = (f32[1,256,512]{2,1,0:T(8,128)S(1)}, f32[1,256,512]{2,1,0:T(8,128)S(1)}, u32[]{:S(2)}, u32[]{:S(2)}) collective-permute-start(f32[1,256,512]{2,1,0:T(8,128)S(1)} %get-tuple-element.5), channel_id=1, source_target_pairs={{0,4},{4,8},{8,12},{12,16},{16,20},{20,24},{24,28},{1,5},{5,9},{9,... | collective-permute-start | bytes 1572872 | tf_op jit(solution)/shard_map/ppermute | solution.py:18
  54.7 0.0 collective-permute-done.9
  54.7 1.6 collective-permute-start.10
  56.3 0.0 collective-permute-done.5
  56.3 0.0 collective-permute-done.4
  56.3 10.0 %multiply_add_fusion.1 = f32[8,256,512]{2,1,0:T(8,128)S(1)} fusion(f32[8,256,512]{2,1,0:T(8,128)} %copy-done.1, f32[1,256,512]{2,1,0:T(8,128)S(1)} %collective-permute-done.5, f32[1,256,512]{2,1,0:T(8,128)S(1)} %collective-permute-done.4), kind=kLoop, calls=%fused_computation.17 | loop fusion | flops 28311552 | bytes 9437184 | tf_op jit(solution)/shard_map/add | solution.py:36
  66.3 0.0 copy-start.3
  66.3 0.1 fusion.18
  66.4 1.4 collective-permute-start.7
  67.8 9.6 %collective-permute-start.6 = (f32[1,256,512]{2,1,0:T(8,128)S(1)}, f32[1,256,512]{2,1,0:T(8,128)S(1)}, u32[]{:S(2)}, u32[]{:S(2)}) collective-permute-start(f32[1,256,512]{2,1,0:T(8,128)S(1)} %get-tuple-element.3), channel_id=1, source_target_pairs={{0,4},{4,8},{8,12},{12,16},{16,20},{20,24},{24,28},{1,5},{5,9},{9,... | collective-permute-start | bytes 1572872 | tf_op jit(solution)/shard_map/ppermute | solution.py:18
  77.5 0.0 collective-permute-done.10
  77.6 0.0 copy-done.3
  77.8 0.0 copy-start.2
  77.9 1.9 fusion.9
  79.7 0.0 collective-permute-done.7
  79.8 0.0 collective-permute-done.6
  79.8 4.6 %multiply_add_fusion = f32[8,256,512]{2,1,0:T(8,128)S(1)} fusion(f32[8,256,512]{2,1,0:T(8,128)S(1)} %multiply_add_fusion.1, f32[1,256,512]{2,1,0:T(8,128)S(1)} %collective-permute-done.7, f32[1,256,512]{2,1,0:T(8,128)S(1)} %collective-permute-done.6), kind=kLoop, calls=%fused_computation.16 | loop fusion | flops 28311552 | bytes 9437184 | tf_op jit(solution)/shard_map/add | solution.py:36
  84.3 0.0 copy-start
  84.3 0.0 copy-done.2
  84.4 2.0 copy-done
  86.4 0.0 copy-start.4
  86.4 3.7 %fusion.11 = f32[256,512]{1,0:T(8,128)S(1)} fusion(f32[2048,512]{1,0:T(8,128)S(1)} %bitcast.7, f32[512,2048]{1,0:T(8,128)S(1)} %constant_dynamic-update-slice_fusion, s32[]{:T(128)S(6)} %select_n.14), kind=kOutput, calls=%fused_computation.25 | convolution fusion | flops 3221225472 | bytes 6815748 | tf_op jit(solution)/shard_map/dot_general | solution.py:40
  90.1 0.9 pad_maximum_fusion.9
  91.0 0.0 reduce-scatter.3.cloned.1.call-update
  91.0 0.0 reduce-scatter.5.cloned.1.call-start
  91.1 0.0 copy-done.4
  91.1 26.5 %all_gather.6 = f32[256,512]{1,0:T(8,128)S(1)} all-gather(f32[32,512]{1,0:T(8,128)S(1)} %copy-done.4), channel_id=1, replica_groups=mesh['pix'=8,'tm'=4] {'pix'}, dimensions={0}, use_global_device_ids=true | all-gather | bytes 589824 | tf_op jit(solution)/shard_map/all_gather | solution.py:69
  117.6 25.6 %reduce-scatter.3.cloned.1.call-done = f32[32,768]{1,0:T(8,128)} async-done(((f32[256,768]{1,0:T(8,128)}), f32[32,768]{1,0:T(8,128)}) %reduce-scatter.3.cloned.1.call-update) | async-done | bytes 98320 | tf_op jit(solution)/shard_map/reduce_scatter | solution.py:71
  143.2 1.3 convolution_divide_fusion.1
  144.4 0.0 copy-start.5
  144.4 10.0 %all_gather.7 = f32[256,512]{1,0:T(8,128)S(1)} all-gather(f32[32,512]{1,0:T(8,128)S(1)} %convolution_divide_fusion.1), channel_id=1, replica_groups=mesh['pix'=8,'tm'=4] {'pix'}, dimensions={0}, use_global_device_ids=true | all-gather | bytes 589824 | tf_op jit(solution)/shard_map/all_gather | solution.py:80
  154.5 0.6 fusion.23
  155.1 5.5 %fusion.22 = f32[256,2048]{1,0:T(8,128)S(1)} fusion(f32[256,512]{1,0:T(8,128)S(1)} %all_gather.7, f32[2048,512]{1,0:T(8,128)} %bitcast.8), kind=kOutput, calls=%fused_computation.48 | convolution fusion | flops 3221225472 | bytes 6815744 | tf_op jit(solution)/shard_map/dot_general | solution.py:44
  160.6 0.0 copy-done.5
  160.6 1.6 pad_maximum_fusion.8
  162.3 0.0 reduce-scatter.5.cloned.1.call-update
  162.3 47.8 %reduce-scatter.5.cloned.1.call-done = f32[64,2304]{1,0:T(8,128)} async-done(((f32[256,2304]{1,0:T(8,128)}), f32[64,2304]{1,0:T(8,128)}) %reduce-scatter.5.cloned.1.call-update) | async-done | bytes 589840 | tf_op jit(solution)/shard_map/reduce_scatter | solution.py:82
  210.1 3.9 %convolution_divide_fusion = f32[64,2048]{1,0:T(8,128)} fusion(f32[512,2048]{1,0:T(8,128)} %copy-done.2, s32[]{:T(128)S(6)} %select_n.14, f32[64,2048]{1,0:T(8,128)S(1)} %copy-done.3, f32[64,2304]{1,0:T(8,128)} %reduce-scatter.5.cloned.1.call-done), kind=kOutput, calls=%fused_computation.21 | convolution fusion | flops 402915328 | bytes 3735556 | tf_op jit(solution)/shard_map/dot_general | solution.py:40
  (8 shorter events, 0.3 us)
Async XLA Ops:
  7.2 136.0 %reduce-scatter.3.cloned.1.call-start = ((), (), s32[]{:S(2)}) async-start(), calls=%async_computation.2 | async-start | bytes 884736 | tf_op jit(solution)/shard_map/reduce_scatter | solution.py:71
  8.5 7.5 %collective-permute-start.1 = (f32[1,256,512]{2,1,0:T(8,128)S(1)}, f32[1,256,512]{2,1,0:T(8,128)S(1)}, u32[]{:S(2)}, u32[]{:S(2)}) collective-permute-start(f32[1,256,512]{2,1,0:T(8,128)S(1)} %get-tuple-element.10), channel_id=1, source_target_pairs={{4,0},{8,4},{12,8},{16,12},{20,16},{24,20},{28,24},{5,1},{9,5},{13... | collective-permute-start | bytes 1572872 | tf_op jit(solution)/shard_map/ppermute | solution.py:20
  9.8 6.2 %collective-permute-start = (f32[1,256,512]{2,1,0:T(8,128)S(1)}, f32[1,256,512]{2,1,0:T(8,128)S(1)}, u32[]{:S(2)}, u32[]{:S(2)}) collective-permute-start(f32[1,256,512]{2,1,0:T(8,128)S(1)} %get-tuple-element.9), channel_id=1, source_target_pairs={{0,4},{4,8},{8,12},{12,16},{16,20},{20,24},{24,28},{1,5},{5,9},{9,... | collective-permute-start | bytes 1572872 | tf_op jit(solution)/shard_map/ppermute | solution.py:18
  12.9 23.5 %collective-permute-start.8 = (f32[64,2048]{1,0:T(8,128)}, f32[64,2048]{1,0:T(8,128)S(1)}, u32[]{:S(2)}, u32[]{:S(2)}) collective-permute-start(f32[64,2048]{1,0:T(8,128)} %param.4), channel_id=1, source_target_pairs={{0,1},{1,2},{2,3},{3,0},{4,5},{5,6},{6,7},{7,4},{8,9},{9,10},{10,1... | collective-permute-start | bytes 1572872 | tf_op jit(solution)/shard_map/ppermute | solution.py:65
  25.9 12.1 %collective-permute-start.3 = (f32[1,256,512]{2,1,0:T(8,128)S(1)}, f32[1,256,512]{2,1,0:T(8,128)S(1)}, u32[]{:S(2)}, u32[]{:S(2)}) collective-permute-start(f32[1,256,512]{2,1,0:T(8,128)S(1)} %get-tuple-element.8), channel_id=1, source_target_pairs={{4,0},{8,4},{12,8},{16,12},{20,16},{24,20},{28,24},{5,1},{9,5},{13... | collective-permute-start | bytes 1572872 | tf_op jit(solution)/shard_map/ppermute | solution.py:20
  27.2 10.8 %collective-permute-start.2 = (f32[1,256,512]{2,1,0:T(8,128)S(1)}, f32[1,256,512]{2,1,0:T(8,128)S(1)}, u32[]{:S(2)}, u32[]{:S(2)}) collective-permute-start(f32[1,256,512]{2,1,0:T(8,128)S(1)} %get-tuple-element.7), channel_id=1, source_target_pairs={{0,4},{4,8},{8,12},{12,16},{16,20},{20,24},{24,28},{1,5},{5,9},{9,... | collective-permute-start | bytes 1572872 | tf_op jit(solution)/shard_map/ppermute | solution.py:18
  36.3 18.3 %collective-permute-start.9 = (f32[64,2048]{1,0:T(8,128)S(1)}, f32[64,2048]{1,0:T(8,128)S(1)}, u32[]{:S(2)}, u32[]{:S(2)}) collective-permute-start(f32[64,2048]{1,0:T(8,128)S(1)} %collective-permute-done.8), channel_id=1, source_target_pairs={{0,1},{1,2},{2,3},{3,0},{4,5},{5,6},{6,7},{7,4},{8,9},{9,10},{10,1... | collective-permute-start | bytes 1572872 | tf_op jit(solution)/shard_map/ppermute | solution.py:65
  42.5 2.0 copy-start.1
  44.6 11.7 %collective-permute-start.5 = (f32[1,256,512]{2,1,0:T(8,128)S(1)}, f32[1,256,512]{2,1,0:T(8,128)S(1)}, u32[]{:S(2)}, u32[]{:S(2)}) collective-permute-start(f32[1,256,512]{2,1,0:T(8,128)S(1)} %get-tuple-element.6), channel_id=1, source_target_pairs={{4,0},{8,4},{12,8},{16,12},{20,16},{24,20},{28,24},{5,1},{9,5},{13... | collective-permute-start | bytes 1572872 | tf_op jit(solution)/shard_map/ppermute | solution.py:20
  45.9 10.4 %collective-permute-start.4 = (f32[1,256,512]{2,1,0:T(8,128)S(1)}, f32[1,256,512]{2,1,0:T(8,128)S(1)}, u32[]{:S(2)}, u32[]{:S(2)}) collective-permute-start(f32[1,256,512]{2,1,0:T(8,128)S(1)} %get-tuple-element.5), channel_id=1, source_target_pairs={{0,4},{4,8},{8,12},{12,16},{16,20},{20,24},{24,28},{1,5},{5,9},{9,... | collective-permute-start | bytes 1572872 | tf_op jit(solution)/shard_map/ppermute | solution.py:18
  54.7 22.8 %collective-permute-start.10 = (f32[64,2048]{1,0:T(8,128)S(1)}, f32[64,2048]{1,0:T(8,128)S(1)}, u32[]{:S(2)}, u32[]{:S(2)}) collective-permute-start(f32[64,2048]{1,0:T(8,128)S(1)} %collective-permute-done.9), channel_id=1, source_target_pairs={{0,1},{1,2},{2,3},{3,0},{4,5},{5,6},{6,7},{7,4},{8,9},{9,10},{10,1... | collective-permute-start | bytes 1572872 | tf_op jit(solution)/shard_map/ppermute | solution.py:65
  66.3 11.3 %copy-start.3 = (f32[64,2048]{1,0:T(8,128)S(1)}, f32[64,2048]{1,0:T(8,128)}, u32[]{:S(2)}) copy-start(f32[64,2048]{1,0:T(8,128)} %param.4) | copy-start | bytes 1572868
  66.4 13.3 %collective-permute-start.7 = (f32[1,256,512]{2,1,0:T(8,128)S(1)}, f32[1,256,512]{2,1,0:T(8,128)S(1)}, u32[]{:S(2)}, u32[]{:S(2)}) collective-permute-start(f32[1,256,512]{2,1,0:T(8,128)S(1)} %get-tuple-element.4), channel_id=1, source_target_pairs={{4,0},{8,4},{12,8},{16,12},{20,16},{24,20},{28,24},{5,1},{9,5},{13... | collective-permute-start | bytes 1572872 | tf_op jit(solution)/shard_map/ppermute | solution.py:20
  67.8 11.9 %collective-permute-start.6 = (f32[1,256,512]{2,1,0:T(8,128)S(1)}, f32[1,256,512]{2,1,0:T(8,128)S(1)}, u32[]{:S(2)}, u32[]{:S(2)}) collective-permute-start(f32[1,256,512]{2,1,0:T(8,128)S(1)} %get-tuple-element.3), channel_id=1, source_target_pairs={{0,4},{4,8},{8,12},{12,16},{16,20},{20,24},{24,28},{1,5},{5,9},{9,... | collective-permute-start | bytes 1572872 | tf_op jit(solution)/shard_map/ppermute | solution.py:18
  77.8 6.5 %copy-start.2 = (f32[512,2048]{1,0:T(8,128)}, f32[512,2048]{1,0:T(8,128)S(1)}, u32[]{:S(2)}) copy-start(f32[512,2048]{1,0:T(8,128)S(1)} %constant_dynamic-update-slice_fusion) | copy-start | bytes 12582916
  84.3 2.0 copy-start
  86.4 4.7 %copy-start.4 = (f32[32,512]{1,0:T(8,128)S(1)}, f32[32,512]{1,0:T(8,128)}, u32[]{:S(2)}) copy-start(f32[32,512]{1,0:T(8,128)} %param.5) | copy-start | bytes 196612
  91.0 119.1 %reduce-scatter.5.cloned.1.call-start = ((), (), s32[]{:S(2)}) async-start(), calls=%async_computation.3 | async-start | bytes 2949120 | tf_op jit(solution)/shard_map/reduce_scatter | solution.py:82
  144.4 16.2 %copy-start.5 = (f32[32,512]{1,0:T(8,128)}, f32[32,512]{1,0:T(8,128)S(1)}, u32[]{:S(2)}) copy-start(f32[32,512]{1,0:T(8,128)S(1)} %convolution_divide_fusion.1) | copy-start | bytes 196612
Sparse Core Ops, SparseCore 0:
  91.1 51.9 reduce-scatter.2
  162.4 47.6 reduce-scatter.4
